TPU v7x, 32 devices: a whole 2x2x4 slice. The times are simulated.
32 devices in a mesh: groups: 2 (over y), seq: 4 (over z), blk: 2 (over x), chan: 2 (over core).
Axes of the slice: x: 2, y: 2, z: 4, core: 2. Of those that a mesh axis runs over, the one named last changes fastest.
Arguments:
- queries: bfloat16 [4, 8, 32, 4096], P(('groups', 'blk'), 'seq', 'chan'), parts along dimension 0, may hold values from -8 to 8
- keys: bfloat16 [4, 8, 32, 4096], P(('groups', 'blk'), 'seq', 'chan'), parts along dimension 0, may hold values from -8 to 8
- values: bfloat16 [4, 8, 32, 4096], P(('groups', 'blk'), 'seq', 'chan'), parts along dimension 0, may hold values from -16 to 16
- norm_gain: float32 [4096], replicated, may hold values from 0.1 to 1.9
- head_weight: bfloat16 [4096, 64], replicated, may hold values from -0.09375 to 0.09375
- head_bias: float32 [64], replicated, may hold values from -3 to 3
- in_weight: bfloat16 [3, 3, 64, 512], replicated, may hold values from -0.25 to 0.25
- in_bias: float32 [512], replicated, may hold values from -3 to 3
- conv_weight: bfloat16 [3, 3, 512, 512], P(None, None, None, 'chan'), may hold values from -0.15625 to 0.15625
- conv_bias: float32 [512], P('chan'), may hold values from -3 to 3
Outputs:
- decoded: bfloat16 [4, 8, 32, 512], P(('groups', 'blk'), 'seq', None, 'chan'), parts along dimension 0
There are 2 independent parts, one for each index of `groups`. A program takes and returns all parts, laid end to end along the dimension named above; an argument that names none is the same for every part. Nothing has to cross between parts.
All inputs are finite; a program needn't handle non-finite values.
Results may differ from a plain program's by a relative error of at most 0.025.
Values may be sent and summed in bfloat16 or wider, within the bound.
A program may use at most 64 MiB of HBM per device.

v0:
```python
import jax
import jax.numpy as jnp
from jax import lax
from jax.sharding import PartitionSpec as P

HD = 128


epsilon = 1e-06


def with_halo(cells, sides, width):
    for axis, dim in sides:
        count = lax.axis_size(axis)
        ends = count - 1
        head = lax.slice_in_dim(cells, 0, width, axis=dim)
        tail = lax.slice_in_dim(cells, cells.shape[dim] - width, cells.shape[dim], axis=dim)
        cells = jnp.concatenate(
            [
                lax.ppermute(tail, axis, [(i, (i + 1) % count) for i in range(ends)]),
                cells,
                lax.ppermute(head, axis, [((i + 1) % count, i) for i in range(ends)]),
            ],
            axis=dim,
        )
    return cells


def conv_valid(inputs, kernel):
    col_count = inputs.shape[2]
    padded = jnp.pad(inputs, ((0, 0), (0, 0), (1, 1), (0, 0)))
    stacked = jnp.concatenate(
        [padded[:, :, col_tap : col_tap + col_count, :] for col_tap in range(3)], axis=-1
    )
    rows_out = inputs.shape[1] - 2
    result = None
    for row_tap in range(3):
        flat_kernel = kernel[row_tap].reshape(3 * kernel.shape[2], kernel.shape[3])
        term = jnp.einsum(
            "frci,io->frco",
            stacked[:, row_tap : row_tap + rows_out],
            flat_kernel,
            preferred_element_type=jnp.float32,
        )
        result = term if result is None else result + term
    return result


def absorb(running, key_block, value_block, query_heads, score_scale):
    run_max, denoms, numers = running
    scores = (
        jnp.einsum("hqd,hkd->hqk", query_heads, key_block, preferred_element_type=jnp.float32)
        * score_scale
    )
    fresh_max = jnp.maximum(run_max, jnp.max(scores, axis=-1))
    rescale = jnp.exp(run_max - fresh_max)
    expo = jnp.exp(scores - fresh_max[..., None])
    denoms = denoms * rescale + jnp.sum(expo, axis=-1)
    numers = numers * rescale[..., None] + jnp.einsum(
        "hqk,hkd->hqd", expo.astype(jnp.bfloat16), value_block, preferred_element_type=jnp.float32
    )
    return (fresh_max, denoms, numers)


def per_device(
    queries,
    keys,
    values,
    norm_gain,
    head_weight,
    head_bias,
    in_weight,
    in_bias,
    conv_weight,
    conv_bias,
):
    frame_dev, rows_dev, cols_dev, feat = queries.shape
    seq_count = lax.axis_size("seq")
    feat_dev = feat // seq_count
    heads_dev = feat_dev // HD
    score_scale = HD ** (-0.5)
    query_all, key_all, value_all = (
        lax.all_to_all(queries, "seq", split_axis=3, concat_axis=1, tiled=True),
        lax.all_to_all(keys, "seq", split_axis=3, concat_axis=1, tiled=True),
        lax.all_to_all(values, "seq", split_axis=3, concat_axis=1, tiled=True),
    )
    all_rows = query_all.shape[1]

    def to_heads(block):
        return block.reshape(-1, heads_dev, HD).transpose(1, 0, 2)

    query_heads = to_heads(query_all)
    key_heads = to_heads(key_all)
    value_heads = to_heads(value_all)
    token_local = query_heads.shape[1]

    def attend_piece(running, block_pair):
        key_piece, value_piece = block_pair
        key_rows = key_piece.shape[1]
        if key_rows > 1024 and key_rows % 1024 == 0:
            count = key_rows // 1024
            key_split = key_piece.reshape(heads_dev, count, 1024, HD).transpose(1, 0, 2, 3)
            value_split = value_piece.reshape(heads_dev, count, 1024, HD).transpose(1, 0, 2, 3)

            def step_block(state, pair_block):
                return (absorb(state, pair_block[0], pair_block[1], query_heads, score_scale), None)

            running, _ = lax.scan(step_block, running, (key_split, value_split))
            return running
        return absorb(running, key_piece, value_piece, query_heads, score_scale)

    start_state = (
        jnp.full((heads_dev, token_local), -1e30, jnp.float32),
        jnp.zeros((heads_dev, token_local), jnp.float32),
        jnp.zeros((heads_dev, token_local, HD), jnp.float32),
    )
    run_max, denoms, numers = attend_piece(
        start_state,
        (
            lax.all_gather(key_heads, ("blk", "chan"), axis=1, tiled=True),
            lax.all_gather(value_heads, ("blk", "chan"), axis=1, tiled=True),
        ),
    )
    attended = (numers / denoms[..., None]).astype(jnp.bfloat16)
    attended = attended.transpose(1, 0, 2).reshape(frame_dev, all_rows, cols_dev, feat_dev)
    back = lax.all_to_all(attended, "seq", split_axis=1, concat_axis=3, tiled=True)
    wide_att = back.astype(jnp.float32)
    squares = jnp.sum(wide_att * wide_att, axis=-1)
    normed = (wide_att * norm_gain).astype(jnp.bfloat16)
    projected = jnp.einsum("frcd,dl->frcl", normed, head_weight, preferred_element_type=jnp.float32)
    rms = jnp.sqrt(squares / feat + epsilon)
    latent_cols = (projected / rms[..., None] + head_bias).astype(jnp.bfloat16)
    latent = lax.all_gather(latent_cols, "chan", axis=2, tiled=True)
    wide_rows = with_halo(latent, (("seq", 1),), 2)
    pre_act = conv_valid(wide_rows, in_weight) + in_bias
    row_ids = lax.axis_index("seq") * rows_dev - 1 + jnp.arange(rows_dev + 2, dtype=jnp.int32)
    inside = (row_ids >= 0) & (row_ids < rows_dev * seq_count)
    activation = jnp.where(inside[None, :, None, None], jax.nn.silu(pre_act), 0.0).astype(
        jnp.bfloat16
    )
    decoded = (conv_valid(activation, conv_weight) + conv_bias).astype(jnp.bfloat16)
    return decoded


def solution(mesh):
    return jax.shard_map(
        per_device,
        mesh=mesh,
        in_specs=(
            P(("groups", "blk"), "seq", "chan", None),
            P(("groups", "blk"), "seq", "chan", None),
            P(("groups", "blk"), "seq", "chan", None),
            P(),
            P(),
            P(),
            P(),
            P(),
            P(None, None, None, "chan"),
            P("chan"),
        ),
        out_specs=P(("groups", "blk"), "seq", None, "chan"),
        check_vma=False,
    )
```

profile of v0, /device:TPU:0, one launch (start us, length us, event | category | flops | bytes accessed | tf_op | source)
XLA Modules:
  0.0 111.8 jit_solution(7479379873750700301)
XLA Ops:
  6.5 4.5 %copy.29 = bf16[1,2,16,4096]{2,1,0,3:T(2,128)(2,1)S(1)} copy(bf16[1,2,16,4096]{3,2,1,0:T(8,128)(2,1)} %param.11) | data formatting | bytes 524288 | tf_op args[1]
  11.1 2.2 %reshape.143 = bf16[4,2,16384]{2,1,0:T(2,128)(2,1)S(1)} reshape(bf16[4096,1,2,16]{3,2,1,0:T(2,128)(2,1)S(1)} %bitcast.113) | data formatting | bytes 524288
  13.3 15.0 %all_to_all.54 = bf16[4,2,16384]{2,1,0:T(2,128)(2,1)S(1)} all-to-all(bf16[4,2,16384]{2,1,0:T(2,128)(2,1)S(1)} %reshape.143), channel_id=1, replica_groups=mesh['groups'=2,'seq'=4,'blk'=2,'chan'=2] {'seq'}, dimensions={0} | all-to-all | bytes 524288 | tf_op jit(solution)/shard_map/all_to_all | solution.py:84
  28.3 1.4 %reshape.144 = bf16[4096,1,2,16]{3,2,1,0:T(2,128)(2,1)S(1)} reshape(bf16[4,2,16384]{2,1,0:T(2,128)(2,1)S(1)} %all_to_all.54) | data formatting | bytes 524288
  31.9 2.7 %copy.32 = bf16[1,2,16,4096]{2,1,0,3:T(2,128)(2,1)S(1)} copy(bf16[1,2,16,4096]{3,2,1,0:T(8,128)(2,1)S(1)} %copy-done.1) | data formatting | bytes 524288 | tf_op args[2]
  34.7 2.2 %reshape.141 = bf16[4,2,16384]{2,1,0:T(2,128)(2,1)S(1)} reshape(bf16[4096,1,2,16]{3,2,1,0:T(2,128)(2,1)S(1)} %bitcast.114) | data formatting | bytes 524288
  36.9 11.0 %all_to_all.55 = bf16[4,2,16384]{2,1,0:T(2,128)(2,1)S(1)} all-to-all(bf16[4,2,16384]{2,1,0:T(2,128)(2,1)S(1)} %reshape.141), channel_id=1, replica_groups=mesh['groups'=2,'seq'=4,'blk'=2,'chan'=2] {'seq'}, dimensions={0} | all-to-all | bytes 524288 | tf_op jit(solution)/shard_map/all_to_all | solution.py:85
  47.8 1.4 %reshape.142 = bf16[4096,1,2,16]{3,2,1,0:T(2,128)(2,1)S(1)} reshape(bf16[4,2,16384]{2,1,0:T(2,128)(2,1)S(1)} %all_to_all.55) | data formatting | bytes 524288
  51.4 2.7 %copy.26 = bf16[1,2,16,4096]{2,1,0,3:T(2,128)(2,1)S(1)} copy(bf16[1,2,16,4096]{3,2,1,0:T(8,128)(2,1)S(1)} %copy-done.2) | data formatting | bytes 524288 | tf_op args[0]
  54.1 2.2 %reshape.145 = bf16[4,2,16384]{2,1,0:T(2,128)(2,1)S(1)} reshape(bf16[4096,1,2,16]{3,2,1,0:T(2,128)(2,1)S(1)} %bitcast.115) | data formatting | bytes 524288
  56.3 11.0 %all_to_all.56 = bf16[4,2,16384]{2,1,0:T(2,128)(2,1)S(1)} all-to-all(bf16[4,2,16384]{2,1,0:T(2,128)(2,1)S(1)} %reshape.145), channel_id=1, replica_groups=mesh['groups'=2,'seq'=4,'blk'=2,'chan'=2] {'seq'}, dimensions={0} | all-to-all | bytes 524288 | tf_op jit(solution)/shard_map/all_to_all | solution.py:83
  67.3 1.4 %reshape.146 = bf16[4096,1,2,16]{3,2,1,0:T(2,128)(2,1)S(1)} reshape(bf16[4,2,16384]{2,1,0:T(2,128)(2,1)S(1)} %all_to_all.56) | data formatting | bytes 524288
  70.1 1.7 %multiply_reduce_fusion = (f32[8,128]{1,0:T(8,128)S(1)}, f32[8,128,512]{2,1,0:T(8,128)S(1)}) fusion(bf16[8,512,128]{2,1,0:T(8,128)(2,1)} %all-gather.4.cloned.1.call-done, bf16[128,8,128]{2,1,0:T(8,128)(2,1)S(1)} %bitcast.127), kind=kOutput, calls=%fused_computation.1 | convolution fusion | flops 135265280 | bytes 3411968 | tf_op jit(solution)/shard_map/hqd,hkd->hqk/dot_general | solution.py:52
  72.5 1.9 %fusion.4 = bf16[128,8,128]{2,0,1:T(8,128)(2,1)S(1)} fusion(bf16[8,512,128]{2,1,0:T(8,128)(2,1)} %all-gather.6.cloned.1.call-done, f32[8,128,512]{2,1,0:T(8,128)S(1)} %get-tuple-element.18, f32[8,128]{1,0:T(8,128)S(1)} %get-tuple-element.16, f32[128,8]{0,1:T(8,128)S(1)} %bitcast_add_fusion, f32[128,8]{0,1:T(8,128)S(1)} %get-tuple-element.15), kind=kOutput, calls=%fused_computation.7 | convolution fusion | flops 136183808 | bytes 3420160 | tf_op jit(solution)/shard_map/hqk,hkd->hqd/dot_general | solution.py:59
  75.4 3.4 %all-to-all-start.3 = ((bf16[1,8,16,1024]{3,2,0,1:T(8,128)(2,1)}), bf16[1,8,16,1024]{3,2,0,1:T(8,128)(2,1)S(1)}, u32[]{:S(2)}, u32[]{:S(2)}) async-start(bf16[1,8,16,1024]{3,2,0,1:T(8,128)(2,1)} %bitcast.12), calls=%async_computation.3 | async-start | bytes 524288 | tf_op jit(solution)/shard_map/all_to_all | solution.py:126
  78.8 1.8 %fusion.30 = (bf16[1,3,64,512]{3,2,1,0:T(8,128)(2,1)}, bf16[1,3,64,512]{3,2,1,0:T(8,128)(2,1)S(1)}, bf16[1,3,64,512]{3,2,1,0:T(8,128)(2,1)S(1)}) fusion(bf16[3,3,64,512]{3,2,1,0:T(8,128)(2,1)} %param.16), kind=kLoop, calls=%fused_computation.60 | loop fusion | bytes 1179648 | tf_op jit(solution)/shard_map/slice | solution.py:38
  80.6 1.8 %fusion.29 = (bf16[1,3,512,256]{3,2,1,0:T(8,128)(2,1)S(1)}, bf16[1,3,512,256]{3,2,1,0:T(8,128)(2,1)S(1)}, bf16[1,3,512,256]{3,2,1,0:T(8,128)(2,1)S(1)}) fusion(bf16[3,3,512,256]{3,2,1,0:T(8,128)(2,1)} %param.18), kind=kLoop, calls=%fused_computation.59 | loop fusion | bytes 4718592 | tf_op jit(solution)/shard_map/slice | solution.py:38
  82.4 4.3 %all-to-all-done.3 = bf16[1,8,16,1024]{3,2,0,1:T(8,128)(2,1)S(1)} async-done(((bf16[1,8,16,1024]{3,2,0,1:T(8,128)(2,1)}), bf16[1,8,16,1024]{3,2,0,1:T(8,128)(2,1)S(1)}, u32[]{:S(2)}, u32[]{:S(2)}) %all-to-all-start.3) | async-done | bytes 262176 | tf_op jit(solution)/shard_map/all_to_all | solution.py:126
  87.9 2.2 %reshape.131 = f32[2,16,4096]{2,1,0:T(8,128)} reshape(f32[1,2,16,4,1024]{4,3,2,1,0:T(4,128)} %copy.38) | data formatting | bytes 1048576 | tf_op jit(solution)/shard_map/convert_element_type | solution.py:127
  91.6 1.4 %fusion.10 = bf16[2,16,64]{2,1,0:T(8,128)(2,1)S(1)} fusion(bf16[4096,64]{0,1:T(8,128)(2,1)S(1)} %copy-done, f32[2,16,4096]{2,1,0:T(8,128)} %reshape.131, f32[4096]{0:T(1024)S(1)} %copy-done.4, f32[64]{0:T(128)} %param.15, f32[2,16]{1,0:T(2,128)S(1)} %add_sqrt_fusion), kind=kOutput, calls=%fused_computation.18 | convolution fusion | flops 17045504 | bytes 1069440 | tf_op jit(solution)/shard_map/frcd,dl->frcl/dot_general | solution.py:130
  93.0 1.8 %all-gather = bf16[2,32,64]{2,1,0:T(8,128)(2,1)S(1)} all-gather(bf16[2,16,64]{2,1,0:T(8,128)(2,1)S(1)} %fusion.10), channel_id=2, replica_groups=mesh['groups'=2,'seq'=4,'blk'=2,'chan'=2] {'chan'}, dimensions={1}, use_global_device_ids=true | all-gather | bytes 12288 | tf_op jit(solution)/shard_map/all_gather | solution.py:133
  94.8 2.2 %collective-permute-start = (bf16[1,2,32,64]{3,2,1,0:T(8,128)(2,1)S(1)}, bf16[1,2,32,64]{3,2,1,0:T(8,128)(2,1)S(1)}, u32[]{:S(2)}, u32[]{:S(2)}) collective-permute-start(bf16[1,2,32,64]{3,2,1,0:T(8,128)(2,1)S(1)} %bitcast.131), channel_id=1, source_target_pairs={{0,4},{4,8},{8,12},{1,5},{5,9},{9,13},{2,6},{6,10},{10,14},{3,7},{... | collective-permute-start | bytes 24584 | tf_op jit(solution)/shard_map/ppermute | solution.py:20
  97.0 1.3 %collective-permute-start.1 = (bf16[1,2,32,64]{3,2,1,0:T(8,128)(2,1)S(1)}, bf16[1,2,32,64]{3,2,1,0:T(8,128)(2,1)S(1)}, u32[]{:S(2)}, u32[]{:S(2)}) collective-permute-start(bf16[1,2,32,64]{3,2,1,0:T(8,128)(2,1)S(1)} %bitcast.132), channel_id=1, source_target_pairs={{4,0},{8,4},{12,8},{5,1},{9,5},{13,9},{6,2},{10,6},{14,10},{7,3},{... | collective-permute-start | bytes 24584 | tf_op jit(solution)/shard_map/ppermute | solution.py:22
  98.5 4.2 %collective-permute-done.1 = bf16[1,2,32,64]{3,2,1,0:T(8,128)(2,1)S(1)} collective-permute-done((bf16[1,2,32,64]{3,2,1,0:T(8,128)(2,1)S(1)}, bf16[1,2,32,64]{3,2,1,0:T(8,128)(2,1)S(1)}, u32[]{:S(2)}, u32[]{:S(2)}) %collective-permute-start.1) | collective-permute-done | bytes 8224 | tf_op jit(solution)/shard_map/ppermute | solution.py:22
  (51 shorter events, 12.1 us)
Async XLA Ops:
  6.5 85.0 %copy-start = (bf16[4096,64]{0,1:T(8,128)(2,1)S(1)}, bf16[4096,64]{0,1:T(8,128)(2,1)}, u32[]{:S(2)}) copy-start(bf16[4096,64]{0,1:T(8,128)(2,1)} %param.14) | copy-start | bytes 1572868
  6.5 63.5 %all-gather.4.cloned.1.call-start = ((), (), s32[]{:S(2)}) async-start(), calls=%async_computation.4 | async-start | bytes 1310720 | tf_op jit(solution)/shard_map/all_gather | solution.py:120
  29.8 2.1 %copy-start.1 = (bf16[1,2,16,4096]{3,2,1,0:T(8,128)(2,1)S(1)}, bf16[1,2,16,4096]{3,2,1,0:T(8,128)(2,1)}, u32[]{:S(2)}) copy-start(bf16[1,2,16,4096]{3,2,1,0:T(8,128)(2,1)} %param.12) | copy-start | bytes 786436
  31.8 40.6 %all-gather.6.cloned.1.call-start = ((), (), s32[]{:S(2)}) async-start(), calls=%async_computation.5 | async-start | bytes 1310720 | tf_op jit(solution)/shard_map/all_gather | solution.py:121
  49.3 2.1 %copy-start.2 = (bf16[1,2,16,4096]{3,2,1,0:T(8,128)(2,1)S(1)}, bf16[1,2,16,4096]{3,2,1,0:T(8,128)(2,1)}, u32[]{:S(2)}) copy-start(bf16[1,2,16,4096]{3,2,1,0:T(8,128)(2,1)} %param.10) | copy-start | bytes 786436
  75.4 11.4 %all-to-all-start.3 = ((bf16[1,8,16,1024]{3,2,0,1:T(8,128)(2,1)}), bf16[1,8,16,1024]{3,2,0,1:T(8,128)(2,1)S(1)}, u32[]{:S(2)}, u32[]{:S(2)}) async-start(bf16[1,8,16,1024]{3,2,0,1:T(8,128)(2,1)} %bitcast.12), calls=%async_computation.3 | async-start | bytes 524288 | tf_op jit(solution)/shard_map/all_to_all | solution.py:126
  82.4 9.2 %copy-start.4 = (f32[4096]{0:T(1024)S(1)}, f32[4096]{0:T(1024)}, u32[]{:S(2)}) copy-start(f32[4096]{0:T(1024)} %param.13) | copy-start | bytes 49156
  90.8 12.4 %copy-start.6 = (f32[512]{0:T(512)S(1)}, f32[512]{0:T(512)}, u32[]{:S(2)}) copy-start(f32[512]{0:T(512)} %param.17) | copy-start | bytes 6148
  91.6 11.7 %copy-start.3 = (bf16[1,3,64,512]{3,2,1,0:T(8,128)(2,1)S(1)}, bf16[1,3,64,512]{3,2,1,0:T(8,128)(2,1)}, u32[]{:S(2)}) copy-start(bf16[1,3,64,512]{3,2,1,0:T(8,128)(2,1)} %get-tuple-element.8) | copy-start | bytes 589828
  94.8 3.7 %collective-permute-start = (bf16[1,2,32,64]{3,2,1,0:T(8,128)(2,1)S(1)}, bf16[1,2,32,64]{3,2,1,0:T(8,128)(2,1)S(1)}, u32[]{:S(2)}, u32[]{:S(2)}) collective-permute-start(bf16[1,2,32,64]{3,2,1,0:T(8,128)(2,1)S(1)} %bitcast.131), channel_id=1, source_target_pairs={{0,4},{4,8},{8,12},{1,5},{5,9},{9,13},{2,6},{6,10},{10,14},{3,7},{... | collective-permute-start | bytes 24584 | tf_op jit(solution)/shard_map/ppermute | solution.py:20
  97.0 5.6 %collective-permute-start.1 = (bf16[1,2,32,64]{3,2,1,0:T(8,128)(2,1)S(1)}, bf16[1,2,32,64]{3,2,1,0:T(8,128)(2,1)S(1)}, u32[]{:S(2)}, u32[]{:S(2)}) collective-permute-start(bf16[1,2,32,64]{3,2,1,0:T(8,128)(2,1)S(1)} %bitcast.132), channel_id=1, source_target_pairs={{4,0},{8,4},{12,8},{5,1},{9,5},{13,9},{6,2},{10,6},{14,10},{7,3},{... | collective-permute-start | bytes 24584 | tf_op jit(solution)/shard_map/ppermute | solution.py:22
  103.2 0.9 copy-start.5
Sparse Core Ops, SparseCore 0:
  32.0 15.7 all-gather.3
  51.5 15.7 all-gather.5
where the time goes:
time: 113 us; the launch traced here: 112 us
  blocking collectives  38.8 us (34%)
  local copies, waits for them, and re-layouts  34.3 us (30%)
  between operations  13.8 us (12%)
  waiting for transfers between devices  8.74 us (8%)
  matrix products  7.01 us (6%)
  starting transfers between devices  6.99 us (6%)
  other arithmetic  2.25 us (2%)
    unnamed x26, local copies, waits for them, and re-layouts  21.1 us
    all_to_all x1, blocking collectives, per_device(): lax.all_to_all(keys, 'seq', split_axis=3, concat_axis=1, tiled=True)  15 us
    all_to_all x1, blocking collectives, per_device(): lax.all_to_all(values, 'seq', split_axis=3, concat_axis=1, tiled=True)  11 us
    all_to_all x1, blocking collectives, per_device(): lax.all_to_all(queries, 'seq', split_axis=3, concat_axis=1, tiled=True)  11 us
    all_to_all x1, waiting for transfers between devices, per_device(): lax.all_to_all(attended, 'seq', split_axis=1, concat_axis=3, tiled=True)  4.35 us
    ppermute x1, waiting for transfers between devices, with_halo(): lax.ppermute(head, axis, [((i + 1) % count, i) for i in range(ends)])  4.21 us
    slice x2, local copies, waits for them, and re-layouts, conv_valid(): flat_kernel = kernel[row_tap].reshape(3 * kernel.shape[2], kernel.shape[3])  3.6 us
    all_to_all x1, starting transfers between devices, per_device(): lax.all_to_all(attended, 'seq', split_axis=1, concat_axis=3, tiled=True)  3.4 us
  transfers between devices with their start and end apart: 5, of which 3 were waited for; matrix products, arithmetic and copies ran while one was open for 20% of the time, Pallas kernels for 0%

commit v1 on v0

--- a/solution.py
+++ b/solution.py
@@ -1,9 +1,15 @@
+import functools
+
 import jax
 import jax.numpy as jnp
 from jax import lax
+from jax.experimental import pallas as pl
+from jax.experimental.pallas import tpu as pltpu
 from jax.sharding import PartitionSpec as P
 
 HD = 128
+LOG2E = 1.4426950408889634
+MESH = pl.DeviceIdType.MESH
 
 
 epsilon = 1e-06
@@ -142,22 +148,418 @@
     return decoded
 
 
+def part_kernel(
+    sizes,
+    q_hbm,
+    k_hbm,
+    v_hbm,
+    gain_hbm,
+    head_hbm,
+    hbias_hbm,
+    win_hbm,
+    bin_hbm,
+    wconv_hbm,
+    bconv_hbm,
+    out_ref,
+    q_buf,
+    k_buf,
+    v_buf,
+    probs,
+    denom,
+    stage,
+    parts,
+    lat_out,
+    lat_buf,
+    gain,
+    head,
+    hbias,
+    win,
+    bin_,
+    wconv,
+    bconv,
+    send_sem,
+    recv_sem,
+    local_sem,
+    part_send,
+    part_recv,
+    lat_send,
+    lat_recv,
+):
+    seq_count, blk_count, chan_count, feat = sizes
+    count = seq_count * blk_count * chan_count
+    _, rows_dev, cols_dev, width = q_buf.shape
+    heads_dev = width // HD
+    tokens_dev = rows_dev * cols_dev
+    tokens = count * tokens_dev
+    lat = hbias.shape[1]
+    seq, blk, chan = lax.axis_index("seq"), lax.axis_index("blk"), lax.axis_index("chan")
+    me = (seq * blk_count + blk) * chan_count + chan
+
+    def at_rank(rank):
+        return {
+            "seq": rank // (blk_count * chan_count),
+            "blk": (rank // chan_count) % blk_count,
+            "chan": rank % chan_count,
+        }
+
+    def ahead(step):
+        return lax.rem(me + step, count)
+
+    own = pl.ds(pl.multiple_of(me * width, HD), width)
+    locals_ = [
+        pltpu.make_async_copy(src, dst, local_sem.at[i])
+        for i, (src, dst) in enumerate(
+            [
+                (q_hbm.at[0, :, :, own], q_buf.at[0]),
+                (k_hbm.at[0, :, :, own], k_buf.at[0]),
+                (v_hbm.at[0, :, :, own], v_buf.at[0]),
+                (gain_hbm.at[:, own], gain),
+                (head_hbm.at[own, :], head),
+                (hbias_hbm, hbias),
+                (win_hbm, win),
+                (bin_hbm, bin_),
+                (wconv_hbm, wconv),
+                (bconv_hbm, bconv),
+            ]
+        )
+    ]
+
+    barrier = pltpu.get_barrier_semaphore()
+    for step in range(1, count):
+        pl.semaphore_signal(barrier, inc=1, device_id=at_rank(ahead(step)), device_id_type=MESH)
+    for copy in locals_:
+        copy.start()
+    pl.semaphore_wait(barrier, count - 1)
+
+    order = sorted(range(1, count), key=lambda step: abs(step - count / 2))
+    tensors = ((q_hbm, q_buf), (k_hbm, k_buf), (v_hbm, v_buf))
+    copies = [{}, {}, {}]
+    for group in ((0, 1), (2,)):
+        for step in order:
+            peer = ahead(step)
+            columns = pl.ds(pl.multiple_of(peer * width, HD), width)
+            for which in group:
+                src, dst = tensors[which]
+                copy = pltpu.make_async_remote_copy(
+                    src_ref=src.at[0, :, :, columns],
+                    dst_ref=dst.at[step],
+                    send_sem=send_sem.at[which, step],
+                    recv_sem=recv_sem.at[which, step],
+                    device_id=at_rank(peer),
+                    device_id_type=MESH,
+                )
+                copy.start()
+                copies[which][step] = copy
+
+    @pl.when(seq == 0)
+    def _():
+        lat_buf[0] = jnp.zeros(lat_buf.shape[1:], lat_buf.dtype)
+
+    @pl.when(seq == seq_count - 1)
+    def _():
+        lat_buf[2] = jnp.zeros(lat_buf.shape[1:], lat_buf.dtype)
+
+    for which in (0, 1):
+        locals_[which].wait()
+        for step in order:
+            copies[which][step].wait_recv()
+
+    slots = max(1, min(count, 128 // tokens_dev))
+    while count % slots:
+        slots -= 1
+    block = slots * tokens_dev
+    scale = HD ** (-0.5) * LOG2E
+    for head_id in range(heads_dev):
+        lanes = slice(head_id * HD, (head_id + 1) * HD)
+        key_head = k_buf[:, :, :, lanes].reshape(tokens, HD)
+        for start in range(0, count, slots):
+            query = q_buf[start : start + slots, :, :, lanes].reshape(block, HD)
+            scores = lax.dot_general(
+                query, key_head, (((1,), (1,)), ((), ())), preferred_element_type=jnp.float32
+            )
+            top = jnp.max(scores, axis=-1, keepdims=True)
+            expo = jnp.exp2((scores - top) * scale)
+            rows = slice(start * tokens_dev, start * tokens_dev + block)
+            denom[head_id, rows, :] = jnp.sum(expo, axis=-1, keepdims=True)
+            probs[head_id, rows, :] = expo.astype(jnp.bfloat16)
+
+    for index in range(2, len(locals_)):
+        locals_[index].wait()
+    for step in order:
+        copies[2][step].wait_recv()
+
+    lane = lax.broadcasted_iota(jnp.int32, (block, 2 * lat), 1)
+    returns = {}
+    gain_row = gain[...]
+    for start in range(0, count, slots):
+        rows = slice(start * tokens_dev, start * tokens_dev + block)
+        total = jnp.zeros((block, 2 * lat), jnp.float32)
+        squares = jnp.zeros((block, 1), jnp.float32)
+        for head_id in range(heads_dev):
+            lanes = slice(head_id * HD, (head_id + 1) * HD)
+            value_head = v_buf[:, :, :, lanes].reshape(tokens, HD)
+            numer = jnp.dot(
+                probs[head_id, rows, :], value_head, preferred_element_type=jnp.float32
+            )
+            attended = (numer / denom[head_id, rows, :]).astype(jnp.bfloat16).astype(jnp.float32)
+            squares = squares + jnp.sum(attended * attended, axis=-1, keepdims=True)
+            normed = (attended * gain_row[:, lanes]).astype(jnp.bfloat16)
+            weight = head[lanes, :]
+            both = jnp.concatenate([weight, jnp.zeros_like(weight)], axis=-1)
+            total = total + jnp.dot(normed, both, preferred_element_type=jnp.float32)
+        high = squares.astype(jnp.bfloat16).astype(jnp.float32)
+        packed = jnp.where(
+            lane < lat, total, jnp.where(lane < lat + lat // 2, high, squares - high)
+        ).astype(jnp.bfloat16)
+        stage[start : start + slots] = packed.reshape(slots, rows_dev, cols_dev, 2 * lat)
+        for step in range(start, start + slots):
+            if step == 0:
+                continue
+            copy = pltpu.make_async_remote_copy(
+                src_ref=stage.at[step],
+                dst_ref=parts.at[step],
+                send_sem=part_send.at[step],
+                recv_sem=part_recv.at[step],
+                device_id=at_rank(ahead(count - step)),
+                device_id_type=MESH,
+            )
+            copy.start()
+            returns[step] = copy
+
+    for copy in returns.values():
+        copy.wait_recv()
+    total = stage[0].astype(jnp.float32)
+    for step in range(1, count):
+        total = total + parts[step].astype(jnp.float32)
+    total = total.reshape(tokens_dev, 2 * lat)
+    squares = total[:, lat : lat + 1] + total[:, lat + lat // 2 : lat + lat // 2 + 1]
+    rms = jnp.sqrt(squares / feat + epsilon)
+    low_lane = lax.broadcasted_iota(jnp.int32, total.shape, 1) < lat
+    twice = jnp.where(low_lane, total, pltpu.roll(total, lat, 1))
+    bias = hbias[...]
+    latent = (twice / rms + jnp.concatenate([bias, bias], axis=-1)).astype(jnp.bfloat16)
+    latent = latent.reshape(rows_dev, cols_dev, 2 * lat)
+    lat_out[...] = latent
+    lat_buf[1, chan] = latent
+
+    def lat_copy(shift, turn):
+        return pltpu.make_async_remote_copy(
+            src_ref=lat_out,
+            dst_ref=lat_buf.at[1 - shift, chan],
+            send_sem=lat_send.at[1 - shift, turn],
+            recv_sem=lat_recv.at[1 - shift, turn],
+            device_id={"seq": seq + shift, "blk": blk, "chan": lax.rem(chan + turn, chan_count)},
+            device_id_type=MESH,
+        )
+
+    def lat_wait(shift, turn):
+        source = lax.rem(chan + chan_count - turn, chan_count)
+        pltpu.make_async_remote_copy(
+            src_ref=lat_out,
+            dst_ref=lat_buf.at[1 - shift, source],
+            send_sem=lat_send.at[1 - shift, turn],
+            recv_sem=lat_recv.at[1 - shift, turn],
+            device_id={"seq": seq, "blk": blk, "chan": chan},
+            device_id_type=MESH,
+        ).wait_recv()
+
+    @pl.when(seq < seq_count - 1)
+    def _():
+        for turn in range(chan_count):
+            lat_copy(1, turn).start()
+
+    @pl.when(seq > 0)
+    def _():
+        for turn in range(chan_count):
+            lat_copy(-1, turn).start()
+
+    for turn in range(1, chan_count):
+        lat_copy(0, turn).start()
+
+    for turn in range(1, chan_count):
+        lat_wait(0, turn)
+
+    @pl.when(seq > 0)
+    def _():
+        for turn in range(chan_count):
+            lat_wait(1, turn)
+
+    @pl.when(seq < seq_count - 1)
+    def _():
+        for turn in range(chan_count):
+            lat_wait(-1, turn)
+
+    pieces = []
+    for side in range(3):
+        picked = range(rows_dev - 2, rows_dev) if side == 0 else range(rows_dev if side == 1 else 2)
+        for row in picked:
+            for part in range(chan_count):
+                pieces.append(lat_buf[side, part, row])
+    cols = chan_count * cols_dev
+    cells = jnp.concatenate(pieces, axis=0).astype(jnp.float32)
+
+    def shifted(cells):
+        col = lax.rem(lax.broadcasted_iota(jnp.int32, cells.shape, 0), cols)
+        before = jnp.where(col == 0, 0.0, pltpu.roll(cells, 1, 0))
+        after = jnp.where(col == cols - 1, 0.0, pltpu.roll(cells, cells.shape[0] - 1, 0))
+        return before, after
+
+    before, after = shifted(cells)
+    low_lane = lax.broadcasted_iota(jnp.int32, cells.shape, 1) < lat
+    stacked = jnp.concatenate(
+        [
+            jnp.where(low_lane, before, cells).astype(jnp.bfloat16),
+            after.astype(jnp.bfloat16)[:, :lat],
+        ],
+        axis=-1,
+    )
+    rows_act = rows_dev + 2
+    pre_act = jnp.zeros((rows_act * cols, win.shape[3]), jnp.float32)
+    for tap in range(3):
+        pre_act = pre_act + jnp.dot(
+            stacked[tap * cols : (tap + rows_act) * cols],
+            win[tap].reshape(3 * lat, win.shape[3]),
+            preferred_element_type=jnp.float32,
+        )
+    pre_act = pre_act + bin_[...]
+    row = lax.broadcasted_iota(jnp.int32, pre_act.shape, 0) // cols + (seq * rows_dev - 1)
+    inside = (row >= 0) & (row < rows_dev * seq_count)
+    activation = jnp.where(inside, pre_act / (1.0 + jnp.exp(-pre_act)), 0.0)
+    before, after = shifted(activation)
+    taps = [side.astype(jnp.bfloat16) for side in (before, activation, after)]
+    result = jnp.zeros((rows_dev * cols, wconv.shape[3]), jnp.float32)
+    for tap in range(3):
+        for side in range(3):
+            result = result + jnp.dot(
+                taps[side][tap * cols : (tap + rows_dev) * cols],
+                wconv[tap, side],
+                preferred_element_type=jnp.float32,
+            )
+    result = (result + bconv[...]).astype(jnp.bfloat16)
+    out_ref[0] = result.reshape(rows_dev, cols, wconv.shape[3])
+
+    for which in range(3):
+        for step in order:
+            copies[which][step].wait_send()
+    for copy in returns.values():
+        copy.wait_send()
+    for turn in range(1, chan_count):
+        lat_copy(0, turn).wait_send()
+
+    @pl.when(seq < seq_count - 1)
+    def _():
+        for turn in range(chan_count):
+            lat_copy(1, turn).wait_send()
+
+    @pl.when(seq > 0)
+    def _():
+        for turn in range(chan_count):
+            lat_copy(-1, turn).wait_send()
+
+
+def per_device_kernel(
+    queries,
+    keys,
+    values,
+    norm_gain,
+    head_weight,
+    head_bias,
+    in_weight,
+    in_bias,
+    conv_weight,
+    conv_bias,
+):
+    _, rows_dev, cols_dev, feat = queries.shape
+    seq_count, blk_count, chan_count = (lax.axis_size(a) for a in ("seq", "blk", "chan"))
+    count = seq_count * blk_count * chan_count
+    width = feat // count
+    tokens_dev = rows_dev * cols_dev
+    tokens = count * tokens_dev
+    heads_dev = width // HD
+    lat = head_weight.shape[1]
+    bf16, f32, dma = jnp.bfloat16, jnp.float32, pltpu.SemaphoreType.DMA
+    row = lambda vector: vector.reshape(1, -1)
+    return pl.pallas_call(
+        functools.partial(part_kernel, (seq_count, blk_count, chan_count, feat)),
+        out_shape=jax.ShapeDtypeStruct(
+            (1, rows_dev, cols_dev * chan_count, conv_weight.shape[3]), bf16
+        ),
+        in_specs=[pl.BlockSpec(memory_space=pl.ANY)] * 10,
+        out_specs=pl.BlockSpec(memory_space=pltpu.VMEM),
+        scratch_shapes=[
+            pltpu.VMEM((count, rows_dev, cols_dev, width), bf16),
+            pltpu.VMEM((count, rows_dev, cols_dev, width), bf16),
+            pltpu.VMEM((count, rows_dev, cols_dev, width), bf16),
+            pltpu.VMEM((heads_dev, tokens, tokens), bf16),
+            pltpu.VMEM((heads_dev, tokens, 1), f32),
+            pltpu.VMEM((count, rows_dev, cols_dev, 2 * lat), bf16),
+            pltpu.VMEM((count, rows_dev, cols_dev, 2 * lat), bf16),
+            pltpu.VMEM((rows_dev, cols_dev, 2 * lat), bf16),
+            pltpu.VMEM((3, chan_count, rows_dev, cols_dev, 2 * lat), bf16),
+            pltpu.VMEM((1, width), f32),
+            pltpu.VMEM((width, lat), bf16),
+            pltpu.VMEM((1, lat), f32),
+            pltpu.VMEM(in_weight.shape, bf16),
+            pltpu.VMEM((1, in_bias.shape[0]), f32),
+            pltpu.VMEM(conv_weight.shape, bf16),
+            pltpu.VMEM((1, conv_bias.shape[0]), f32),
+            dma((3, count)),
+            dma((3, count)),
+            dma((10,)),
+            dma((count,)),
+            dma((count,)),
+            dma((3, chan_count)),
+            dma((3, chan_count)),
+        ],
+        compiler_params=pltpu.CompilerParams(collective_id=0, has_side_effects=True),
+        name="part_kernel",
+    )(
+        queries,
+        keys,
+        values,
+        row(norm_gain),
+        head_weight,
+        row(head_bias),
+        in_weight,
+        row(in_bias),
+        conv_weight,
+        row(conv_bias),
+    )
+
+
+def fits_kernel(queries, head_weight, mesh):
+    frames, rows, cols, feat = queries.shape
+    seq_count, blk_count, chan_count = (mesh.shape[a] for a in ("seq", "blk", "chan"))
+    count = seq_count * blk_count * chan_count
+    return (
+        feat % (count * HD) == 0
+        and frames == mesh.shape["groups"] * blk_count
+        and rows // seq_count >= 2
+        and (cols // chan_count) % 16 == 0
+        and 2 * head_weight.shape[1] == 128
+    )
+
+
 def solution(mesh):
-    return jax.shard_map(
-        per_device,
-        mesh=mesh,
-        in_specs=(
-            P(("groups", "blk"), "seq", "chan", None),
-            P(("groups", "blk"), "seq", "chan", None),
-            P(("groups", "blk"), "seq", "chan", None),
-            P(),
-            P(),
-            P(),
-            P(),
-            P(),
-            P(None, None, None, "chan"),
-            P("chan"),
-        ),
-        out_specs=P(("groups", "blk"), "seq", None, "chan"),
-        check_vma=False,
-    )
+    def run(*args):
+        body = per_device_kernel if fits_kernel(args[0], args[4], mesh) else per_device
+        return jax.shard_map(
+            body,
+            mesh=mesh,
+            in_specs=(
+                P(("groups", "blk"), "seq", "chan", None),
+                P(("groups", "blk"), "seq", "chan", None),
+                P(("groups", "blk"), "seq", "chan", None),
+                P(),
+                P(),
+                P(),
+                P(),
+                P(),
+                P(None, None, None, "chan"),
+                P("chan"),
+            ),
+            out_specs=P(("groups", "blk"), "seq", None, "chan"),
+            check_vma=False,
+        )(*args)
+
+    return run

time: 113 us -> 40.3 us (0.36)
  blocking collectives: 38.8 us -> 0 us
  Pallas kernels: 0 us -> 36.3 us
  local copies, waits for them, and re-layouts: 34.3 us -> 3.75 us
  between operations: 13.8 us -> 0.01 us
  waiting for transfers between devices: 8.74 us -> 0 us
  matrix products: 7.01 us -> 0 us
  starting transfers between devices: 6.99 us -> 0 us
  other arithmetic: 2.25 us -> 0 us
    all_to_all x3 -> x0, blocking collectives: 37 us -> none  [the longest x1 15 us: per_device(): lax.all_to_all(keys, 'seq', split_axis=3, concat_axis=1, tiled=True)]
    pallas_call x0 -> x1, Pallas kernels: none -> 36.3 us  [per_device_kernel(): pl.pallas_call(functools.partial(part_kernel, (seq_count, blk_count, chan...]
    unnamed x26 -> x2, local copies, waits for them, and re-layouts: 21.1 us -> 3.75 us
    dot_general x9 -> x0, matrix products: 7.01 us -> none  [the longest x6 2 us: conv_valid(): jnp.einsum('frci,io->frco', stacked[:, row_tap:row_tap + rows_out], flat_...]
    all_to_all x1 -> x0, waiting for transfers between devices: 4.35 us -> none  [per_device(): lax.all_to_all(attended, 'seq', split_axis=1, concat_axis=3, tiled=True)]
    ppermute x2 -> x0, waiting for transfers between devices: 4.32 us -> none  [the longest x1 4.21 us: with_halo(): lax.ppermute(head, axis, [((i + 1) % count, i) for i in range(ends)])]
    all_to_all x3 -> x0, local copies, waits for them, and re-layouts: 3.77 us -> none  [the longest x1 1.26 us: per_device(): lax.all_to_all(keys, 'seq', split_axis=3, concat_axis=1, tiled=True)]
    slice x4 -> x0, local copies, waits for them, and re-layouts: 3.67 us -> none  [the longest x2 3.6 us: conv_valid(): flat_kernel = kernel[row_tap].reshape(3 * kernel.shape[2], kernel.shape[3])]
  transfers between devices with their start and end apart: 5 -> 0, of which waited for: 3 -> 0; matrix products, arithmetic and copies ran while one was open for 20% -> 0% of each run, Pallas kernels for 0% -> 0%
where the time goes in v1:
time: 40.3 us; the launch traced here: 40.1 us
  Pallas kernels  36.3 us (90%)
  local copies, waits for them, and re-layouts  3.75 us (9%)
    pallas_call x1, Pallas kernels, per_device_kernel(): pl.pallas_call(functools.partial(part_kernel, (seq_count, blk_count, chan...  36.3 us
    unnamed x2, local copies, waits for them, and re-layouts  3.75 us

profile of v1, /device:TPU:0, one launch (start us, length us, event | category | flops | bytes accessed | tf_op | source)
XLA Modules:
  0.0 40.1 jit_solution(13899570383376310697)
XLA Ops:
  0.0 2.4 %copy.11.head_hbm = bf16[4096,64]{1,0:T(8,128)(2,1)} copy(bf16[4096,64]{0,1:T(8,128)(2,1)} %param.14) | data formatting | bytes 1048576 | tf_op args[4]
  2.4 36.3 %part_kernel.1 = bf16[1,2,32,256]{3,2,1,0:T(8,128)(2,1)} custom-call(bf16[1,2,16,4096]{3,2,1,0:T(8,128)(2,1)} %q_hbm.1, bf16[1,2,16,4096]{3,2,1,0:T(8,128)(2,1)} %k_hbm.1, bf16[1,2,16,4096]{3,2,1,0:T(8,128)(2,1)} %v_hbm.1, f32[1,4096]{1,0:T(1,128)} %bitcast.4, bf16[4096,64]{1,0:T(8,128)(2,1)} %copy.11.head_hbm, f32[1,64]{1,0:T(1,128)} %bitcast.7, ...), custom_call_target="tpu_custom_call" | custom-call | tf_op jit(solution)/shard_map/part_kernel/pallas_call | solution.py:482
  38.7 1.4 %copy.13 = bf16[1,2,32,256]{3,2,1,0:T(8,128)(2,1)} copy(bf16[1,2,32,256]{3,2,1,0:T(8,128)(2,1)} %part_kernel.1) | data formatting | bytes 65536

commit v2 on v1

--- a/solution.py
+++ b/solution.py
@@ -9,6 +9,7 @@
 
 HD = 128
 LOG2E = 1.4426950408889634
+BLOCK = 128
 MESH = pl.DeviceIdType.MESH
 
 
@@ -164,8 +165,6 @@
     q_buf,
     k_buf,
     v_buf,
-    probs,
-    denom,
     stage,
     parts,
     lat_out,
@@ -184,9 +183,11 @@
     part_recv,
     lat_send,
     lat_recv,
+    ready,
 ):
     seq_count, blk_count, chan_count, feat = sizes
-    count = seq_count * blk_count * chan_count
+    plane = blk_count * chan_count
+    count = seq_count * plane
     _, rows_dev, cols_dev, width = q_buf.shape
     heads_dev = width // HD
     tokens_dev = rows_dev * cols_dev
@@ -197,24 +198,32 @@
 
     def at_rank(rank):
         return {
-            "seq": rank // (blk_count * chan_count),
+            "seq": rank // plane,
             "blk": (rank // chan_count) % blk_count,
             "chan": rank % chan_count,
         }
 
-    def ahead(step):
-        return lax.rem(me + step, count)
+    near_ends = jnp.minimum(seq, seq_count - 1 - seq)
+    upward = jnp.where(seq < seq_count - 1 - seq, 1, -1)
+
+    def by_distance(place):
+        paired = place <= 2 * near_ends
+        dist = jnp.where(paired, (place + 1) // 2, place - near_ends)
+        return dist, jnp.where(paired, 2 * (place % 2) - 1, upward)
+
+    def rank_of(seq_at, turn):
+        return seq_at * plane + lax.rem(me % plane + turn, plane)
 
     own = pl.ds(pl.multiple_of(me * width, HD), width)
     locals_ = [
         pltpu.make_async_copy(src, dst, local_sem.at[i])
         for i, (src, dst) in enumerate(
             [
-                (q_hbm.at[0, :, :, own], q_buf.at[0]),
-                (k_hbm.at[0, :, :, own], k_buf.at[0]),
-                (v_hbm.at[0, :, :, own], v_buf.at[0]),
+                (q_hbm.at[0, :, :, own], q_buf.at[me]),
+                (k_hbm.at[0, :, :, own], k_buf.at[me]),
+                (v_hbm.at[0, :, :, own], v_buf.at[me]),
                 (gain_hbm.at[:, own], gain),
-                (head_hbm.at[own, :], head),
+                (head_hbm.at[:, own], head),
                 (hbias_hbm, hbias),
                 (win_hbm, win),
                 (bin_hbm, bin_),
@@ -225,31 +234,71 @@
     ]
 
     barrier = pltpu.get_barrier_semaphore()
-    for step in range(1, count):
-        pl.semaphore_signal(barrier, inc=1, device_id=at_rank(ahead(step)), device_id_type=MESH)
+
+    def greet(seq_at, first):
+        for turn in range(first, plane):
+            pl.semaphore_signal(
+                barrier, inc=1, device_id=at_rank(rank_of(seq_at, turn)), device_id_type=MESH
+            )
+
+    has_up, has_down = seq < seq_count - 1, seq > 0
+    pl.when(has_up)(lambda: greet(seq + 1, 0))
+    pl.when(has_down)(lambda: greet(seq - 1, 0))
+    greet(seq, 1)
     for copy in locals_:
         copy.start()
-    pl.semaphore_wait(barrier, count - 1)
-
-    order = sorted(range(1, count), key=lambda step: abs(step - count / 2))
-    tensors = ((q_hbm, q_buf), (k_hbm, k_buf), (v_hbm, v_buf))
-    copies = [{}, {}, {}]
-    for group in ((0, 1), (2,)):
-        for step in order:
-            peer = ahead(step)
-            columns = pl.ds(pl.multiple_of(peer * width, HD), width)
-            for which in group:
-                src, dst = tensors[which]
-                copy = pltpu.make_async_remote_copy(
-                    src_ref=src.at[0, :, :, columns],
-                    dst_ref=dst.at[step],
-                    send_sem=send_sem.at[which, step],
-                    recv_sem=recv_sem.at[which, step],
-                    device_id=at_rank(peer),
-                    device_id_type=MESH,
-                )
-                copy.start()
-                copies[which][step] = copy
+    sides = jnp.where(has_up, 1, 0) + jnp.where(has_down, 1, 0)
+    pl.semaphore_wait(barrier, plane - 1 + plane * sides)
+
+    def tell(way, dist):
+        pl.semaphore_signal(
+            ready.at[(way + 1) // 2, dist],
+            inc=1,
+            device_id={"seq": seq - way, "blk": blk, "chan": chan},
+            device_id_type=MESH,
+        )
+
+    if seq_count > 2:
+
+        @pl.when(has_up & has_down)
+        def _():
+            tell(1, 2)
+            tell(-1, 2)
+
+    def moved(which, seq_at, turn, slot):
+        src, dst = ((q_hbm, q_buf), (k_hbm, k_buf), (v_hbm, v_buf))[which]
+        peer = rank_of(seq_at, turn)
+        return pltpu.make_async_remote_copy(
+            src_ref=src.at[0, :, :, pl.ds(pl.multiple_of(peer * width, HD), width)],
+            dst_ref=dst.at[slot],
+            send_sem=send_sem.at[which, peer],
+            recv_sem=recv_sem.at[which, slot],
+            device_id=at_rank(peer),
+            device_id_type=MESH,
+        )
+
+    places = [(seq, 1)]
+    for place in range(1, seq_count):
+        dist, way = by_distance(place)
+        places.append((seq + dist * way, 0))
+    for place, (seq_at, first) in enumerate(places):
+        if place >= 2:
+            dist, way = by_distance(place)
+
+            @pl.when(dist >= 2)
+            def _():
+                pl.semaphore_wait(ready.at[(way + 1) // 2, dist], 1)
+
+                @pl.when((seq - way >= 0) & (seq - way < seq_count))
+                def _():
+                    tell(way, dist + 1)
+
+        for turn in range(first, plane):
+            for which in (1, 2):
+                moved(which, seq_at, turn, me).start()
+    for seq_at, first in places:
+        for turn in range(first, plane):
+            moved(0, seq_at, turn, me).start()
 
     @pl.when(seq == 0)
     def _():
@@ -259,78 +308,96 @@
     def _():
         lat_buf[2] = jnp.zeros(lat_buf.shape[1:], lat_buf.dtype)
 
-    for which in (0, 1):
-        locals_[which].wait()
-        for step in order:
-            copies[which][step].wait_recv()
-
-    slots = max(1, min(count, 128 // tokens_dev))
-    while count % slots:
+    for copy in locals_:
+        copy.wait()
+    for seq_at, first in places:
+        for turn in range(first, plane):
+            for which in (1, 2):
+                moved(which, seq_at, turn, rank_of(seq_at, turn)).wait_recv()
+
+    slots = max(1, min(plane, BLOCK // tokens_dev))
+    while plane % slots:
         slots -= 1
     block = slots * tokens_dev
     scale = HD ** (-0.5) * LOG2E
-    for head_id in range(heads_dev):
-        lanes = slice(head_id * HD, (head_id + 1) * HD)
-        key_head = k_buf[:, :, :, lanes].reshape(tokens, HD)
-        for start in range(0, count, slots):
-            query = q_buf[start : start + slots, :, :, lanes].reshape(block, HD)
+    lane = lax.broadcasted_iota(jnp.int32, (block, 2 * lat), 1)
+    gain_row = gain[...]
+
+    def attend(seq_at, first, begin):
+        start = seq_at * plane + begin
+        for slot in range(begin, begin + slots):
+            peer = seq_at * plane + slot
+
+            @pl.when(peer != me)
+            def _():
+                received(q_buf, recv_sem.at[0, peer], peer).wait_recv()
+
+        total = jnp.zeros((block, 2 * lat), jnp.float32)
+        squares = jnp.zeros((block, 1), jnp.float32)
+        for head_id in range(heads_dev):
+            lanes = slice(head_id * HD, (head_id + 1) * HD)
+            query = q_buf[pl.ds(start, slots), :, :, lanes].reshape(block, HD)
+            key_head = k_buf[:, :, :, lanes].reshape(tokens, HD)
+            value_head = v_buf[:, :, :, lanes].reshape(tokens, HD)
             scores = lax.dot_general(
                 query, key_head, (((1,), (1,)), ((), ())), preferred_element_type=jnp.float32
             )
             top = jnp.max(scores, axis=-1, keepdims=True)
             expo = jnp.exp2((scores - top) * scale)
-            rows = slice(start * tokens_dev, start * tokens_dev + block)
-            denom[head_id, rows, :] = jnp.sum(expo, axis=-1, keepdims=True)
-            probs[head_id, rows, :] = expo.astype(jnp.bfloat16)
-
-    for index in range(2, len(locals_)):
-        locals_[index].wait()
-    for step in order:
-        copies[2][step].wait_recv()
-
-    lane = lax.broadcasted_iota(jnp.int32, (block, 2 * lat), 1)
-    returns = {}
-    gain_row = gain[...]
-    for start in range(0, count, slots):
-        rows = slice(start * tokens_dev, start * tokens_dev + block)
-        total = jnp.zeros((block, 2 * lat), jnp.float32)
-        squares = jnp.zeros((block, 1), jnp.float32)
-        for head_id in range(heads_dev):
-            lanes = slice(head_id * HD, (head_id + 1) * HD)
-            value_head = v_buf[:, :, :, lanes].reshape(tokens, HD)
+            denom = jnp.sum(expo, axis=-1, keepdims=True)
             numer = jnp.dot(
-                probs[head_id, rows, :], value_head, preferred_element_type=jnp.float32
+                expo.astype(jnp.bfloat16), value_head, preferred_element_type=jnp.float32
             )
-            attended = (numer / denom[head_id, rows, :]).astype(jnp.bfloat16).astype(jnp.float32)
+            attended = (numer / denom).astype(jnp.bfloat16).astype(jnp.float32)
             squares = squares + jnp.sum(attended * attended, axis=-1, keepdims=True)
             normed = (attended * gain_row[:, lanes]).astype(jnp.bfloat16)
-            weight = head[lanes, :]
-            both = jnp.concatenate([weight, jnp.zeros_like(weight)], axis=-1)
-            total = total + jnp.dot(normed, both, preferred_element_type=jnp.float32)
+            weight = head[:, lanes]
+            both = jnp.concatenate([weight, jnp.zeros_like(weight)], axis=0)
+            total = total + lax.dot_general(
+                normed, both, (((1,), (1,)), ((), ())), preferred_element_type=jnp.float32
+            )
         high = squares.astype(jnp.bfloat16).astype(jnp.float32)
         packed = jnp.where(
             lane < lat, total, jnp.where(lane < lat + lat // 2, high, squares - high)
         ).astype(jnp.bfloat16)
-        stage[start : start + slots] = packed.reshape(slots, rows_dev, cols_dev, 2 * lat)
-        for step in range(start, start + slots):
-            if step == 0:
-                continue
-            copy = pltpu.make_async_remote_copy(
-                src_ref=stage.at[step],
-                dst_ref=parts.at[step],
-                send_sem=part_send.at[step],
-                recv_sem=part_recv.at[step],
-                device_id=at_rank(ahead(count - step)),
-                device_id_type=MESH,
-            )
-            copy.start()
-            returns[step] = copy
-
-    for copy in returns.values():
-        copy.wait_recv()
-    total = stage[0].astype(jnp.float32)
-    for step in range(1, count):
-        total = total + parts[step].astype(jnp.float32)
+        stage[pl.ds(start, slots)] = packed.reshape(slots, rows_dev, cols_dev, 2 * lat)
+        for slot in range(begin, begin + slots):
+            peer = seq_at * plane + slot
+
+            @pl.when(peer != me)
+            def _():
+                given(peer, me).start()
+
+    def received(buf, sem, peer):
+        return pltpu.make_async_remote_copy(
+            src_ref=buf.at[me],
+            dst_ref=buf.at[peer],
+            send_sem=send_sem.at[0, peer],
+            recv_sem=sem,
+            device_id=at_rank(peer),
+            device_id_type=MESH,
+        )
+
+    def given(peer, slot):
+        return pltpu.make_async_remote_copy(
+            src_ref=stage.at[peer],
+            dst_ref=parts.at[slot],
+            send_sem=part_send.at[peer],
+            recv_sem=part_recv.at[slot],
+            device_id=at_rank(peer),
+            device_id_type=MESH,
+        )
+
+    for seq_at, first in places:
+        for begin in range(0, plane, slots):
+            attend(seq_at, first, begin)
+
+    total = stage[me].astype(jnp.float32)
+    for seq_at, first in places:
+        for turn in range(first, plane):
+            peer = rank_of(seq_at, turn)
+            given(peer, peer).wait_recv()
+            total = total + parts[peer].astype(jnp.float32)
     total = total.reshape(tokens_dev, 2 * lat)
     squares = total[:, lat : lat + 1] + total[:, lat + lat // 2 : lat + lat // 2 + 1]
     rms = jnp.sqrt(squares / feat + epsilon)
@@ -438,11 +505,12 @@
     result = (result + bconv[...]).astype(jnp.bfloat16)
     out_ref[0] = result.reshape(rows_dev, cols, wconv.shape[3])
 
-    for which in range(3):
-        for step in order:
-            copies[which][step].wait_send()
-    for copy in returns.values():
-        copy.wait_send()
+    for seq_at, first in places:
+        for turn in range(first, plane):
+            peer = rank_of(seq_at, turn)
+            for which in range(3):
+                moved(which, seq_at, turn, me).wait_send()
+            given(peer, me).wait_send()
     for turn in range(1, chan_count):
         lat_copy(0, turn).wait_send()
 
@@ -473,15 +541,12 @@
     seq_count, blk_count, chan_count = (lax.axis_size(a) for a in ("seq", "blk", "chan"))
     count = seq_count * blk_count * chan_count
     width = feat // count
-    tokens_dev = rows_dev * cols_dev
-    tokens = count * tokens_dev
-    heads_dev = width // HD
     lat = head_weight.shape[1]
     bf16, f32, dma = jnp.bfloat16, jnp.float32, pltpu.SemaphoreType.DMA
     row = lambda vector: vector.reshape(1, -1)
     return pl.pallas_call(
         functools.partial(part_kernel, (seq_count, blk_count, chan_count, feat)),
-        out_shape=jax.ShapeDtypeStruct(
+        out_shape=pltpu.VMEM(
             (1, rows_dev, cols_dev * chan_count, conv_weight.shape[3]), bf16
         ),
         in_specs=[pl.BlockSpec(memory_space=pl.ANY)] * 10,
@@ -490,14 +555,12 @@
             pltpu.VMEM((count, rows_dev, cols_dev, width), bf16),
             pltpu.VMEM((count, rows_dev, cols_dev, width), bf16),
             pltpu.VMEM((count, rows_dev, cols_dev, width), bf16),
-            pltpu.VMEM((heads_dev, tokens, tokens), bf16),
-            pltpu.VMEM((heads_dev, tokens, 1), f32),
             pltpu.VMEM((count, rows_dev, cols_dev, 2 * lat), bf16),
             pltpu.VMEM((count, rows_dev, cols_dev, 2 * lat), bf16),
             pltpu.VMEM((rows_dev, cols_dev, 2 * lat), bf16),
             pltpu.VMEM((3, chan_count, rows_dev, cols_dev, 2 * lat), bf16),
             pltpu.VMEM((1, width), f32),
-            pltpu.VMEM((width, lat), bf16),
+            pltpu.VMEM((lat, width), bf16),
             pltpu.VMEM((1, lat), f32),
             pltpu.VMEM(in_weight.shape, bf16),
             pltpu.VMEM((1, in_bias.shape[0]), f32),
@@ -510,6 +573,7 @@
             dma((count,)),
             dma((3, chan_count)),
             dma((3, chan_count)),
+            pltpu.SemaphoreType.REGULAR((2, seq_count + 1)),
         ],
         compiler_params=pltpu.CompilerParams(collective_id=0, has_side_effects=True),
         name="part_kernel",
@@ -518,7 +582,7 @@
         keys,
         values,
         row(norm_gain),
-        head_weight,
+        head_weight.T,
         row(head_bias),
         in_weight,
         row(in_bias),

time: 40.3 us -> 34.8 us (0.86)
  local copies, waits for them, and re-layouts: 3.75 us -> 0.62 us
  Pallas kernels: 36.3 us -> 34.1 us
    unnamed x2 -> x1, local copies, waits for them, and re-layouts: 3.75 us -> 0.62 us
    pallas_call x1, Pallas kernels: 36.3 us -> 34.1 us  [per_device_kernel(): pl.pallas_call(functools.partial(part_kernel, (seq_count, blk_count, chan...]
where the time goes in v2:
time: 34.8 us; the launch traced here: 34.7 us
  Pallas kernels  34.1 us (98%)
  local copies, waits for them, and re-layouts  0.62 us (2%)
    pallas_call x1, Pallas kernels, per_device_kernel(): pl.pallas_call(functools.partial(part_kernel, (seq_count, blk_count, chan...  34.1 us

profile of v2, /device:TPU:0, one launch (start us, length us, event | category | flops | bytes accessed | tf_op | source)
XLA Modules:
  0.0 34.7 jit_solution(2454053527002235233)
XLA Ops:
  0.0 34.1 %part_kernel.1 = bf16[1,2,32,256]{3,2,1,0:T(8,128)(2,1)S(1)} custom-call(bf16[1,2,16,4096]{3,2,1,0:T(8,128)(2,1)} %q_hbm.1, bf16[1,2,16,4096]{3,2,1,0:T(8,128)(2,1)} %k_hbm.1, bf16[1,2,16,4096]{3,2,1,0:T(8,128)(2,1)} %v_hbm.1, f32[1,4096]{1,0:T(1,128)} %bitcast.6, bf16[64,4096]{1,0:T(8,128)(2,1)} %bitcast.5, f32[1,64]{1,0:T(1,128)} %bitcast.9, ...), custom_call_target="tpu_custom_call" | custom-call | tf_op jit(solution)/shard_map/part_kernel/pallas_call | solution.py:547
  34.1 0.6 %copy.12 = bf16[1,2,32,256]{3,2,1,0:T(8,128)(2,1)} copy(bf16[1,2,32,256]{3,2,1,0:T(8,128)(2,1)S(1)} %part_kernel.1) | data formatting | bytes 65536

commit v3 on v2

--- a/solution.py
+++ b/solution.py
@@ -209,7 +209,7 @@
     def by_distance(place):
         paired = place <= 2 * near_ends
         dist = jnp.where(paired, (place + 1) // 2, place - near_ends)
-        return dist, jnp.where(paired, 2 * (place % 2) - 1, upward)
+        return dist, jnp.where(paired, upward * (2 * (place % 2) - 1), upward)
 
     def rank_of(seq_at, turn):
         return seq_at * plane + lax.rem(me % plane + turn, plane)
@@ -281,24 +281,26 @@
     for place in range(1, seq_count):
         dist, way = by_distance(place)
         places.append((seq + dist * way, 0))
-    for place, (seq_at, first) in enumerate(places):
-        if place >= 2:
-            dist, way = by_distance(place)
-
-            @pl.when(dist >= 2)
+    def send(which_ones, group):
+        for seq_at, first in group:
+            for turn in range(first, plane):
+                for which in which_ones:
+                    moved(which, seq_at, turn, me).start()
+
+    send((1, 2), places[1:2])
+    for place in range(2, seq_count):
+        dist, way = by_distance(place)
+
+        @pl.when(dist >= 2)
+        def _():
+            pl.semaphore_wait(ready.at[(way + 1) // 2, dist], 1)
+
+            @pl.when((seq - way >= 0) & (seq - way < seq_count))
             def _():
-                pl.semaphore_wait(ready.at[(way + 1) // 2, dist], 1)
-
-                @pl.when((seq - way >= 0) & (seq - way < seq_count))
-                def _():
-                    tell(way, dist + 1)
-
-        for turn in range(first, plane):
-            for which in (1, 2):
-                moved(which, seq_at, turn, me).start()
-    for seq_at, first in places:
-        for turn in range(first, plane):
-            moved(0, seq_at, turn, me).start()
+                tell(way, dist + 1)
+
+    send((1, 2), places[2:] + places[:1])
+    send((0,), places[:1] + places[:0:-1])
 
     @pl.when(seq == 0)
     def _():

time: 34.8 us -> 34.7 us (level)
  no operation moved by 1% of the time
where the time goes in v3:
time: 34.7 us; the launch traced here: 34.5 us
  Pallas kernels  33.9 us (98%)
  local copies, waits for them, and re-layouts  0.62 us (2%)
    pallas_call x1, Pallas kernels, per_device_kernel(): pl.pallas_call(functools.partial(part_kernel, (seq_count, blk_count, chan...  33.9 us

profile of v3, /device:TPU:0, one launch (start us, length us, event | category | flops | bytes accessed | tf_op | source)
XLA Modules:
  0.0 34.5 jit_solution(624486249257872377)
XLA Ops:
  0.0 33.9 %part_kernel.1 = bf16[1,2,32,256]{3,2,1,0:T(8,128)(2,1)S(1)} custom-call(bf16[1,2,16,4096]{3,2,1,0:T(8,128)(2,1)} %q_hbm.1, bf16[1,2,16,4096]{3,2,1,0:T(8,128)(2,1)} %k_hbm.1, bf16[1,2,16,4096]{3,2,1,0:T(8,128)(2,1)} %v_hbm.1, f32[1,4096]{1,0:T(1,128)} %bitcast.6, bf16[64,4096]{1,0:T(8,128)(2,1)} %bitcast.5, f32[1,64]{1,0:T(1,128)} %bitcast.9, ...), custom_call_target="tpu_custom_call" | custom-call | tf_op jit(solution)/shard_map/part_kernel/pallas_call | solution.py:549
  33.9 0.6 %copy.12 = bf16[1,2,32,256]{3,2,1,0:T(8,128)(2,1)} copy(bf16[1,2,32,256]{3,2,1,0:T(8,128)(2,1)S(1)} %part_kernel.1) | data formatting | bytes 65536
